TPU v7x, 256 devices: a whole 4x4x8 slice. The times are simulated.
256 devices in a mesh: ctx: 32 (over z, y_hi, core), head: 8 (over y_lo, x).
Axes of the slice: x: 4, y: 4 (y_hi: 2, y_lo: 2; y = y_hi * 2 + y_lo), z: 8, core: 2. Of those that a mesh axis runs over, the one named last changes fastest.
Arguments:
- query1: bfloat16 [16384, 6144], P('ctx', 'head'), may hold values from -6 to 6
- key1: bfloat16 [16384, 6144], P('ctx', 'head'), may hold values from -6 to 6
- value1: bfloat16 [16384, 6144], P('ctx', 'head'), may hold values from -50 to 50
- log_decay: float32 [16384, 64], P('ctx', 'head'), may hold values from -1 to 0
- out_weight: bfloat16 [6144, 3072], P('head'), may hold values from -0.078125 to 0.078125
- query2: bfloat16 [16384, 6144], P('ctx', 'head'), may hold values from -12 to 12
- key2: bfloat16 [16384, 6144], P('ctx', 'head'), may hold values from -6 to 6
- value2: bfloat16 [16384, 6144], P('ctx', 'head'), may hold values from -6 to 6
Outputs:
- linear_mixed: bfloat16 [16384, 3072], P(('ctx', 'head'))
- attended: bfloat16 [16384, 6144], P('ctx', 'head')
All inputs are finite; a program needn't handle non-finite values.
Results may differ from a plain program's by a relative error of at most 0.017.
Values may be sent and summed in bfloat16 or wider, within the bound.
A program may use at most 64 MiB of HBM per device.

v0:
```python
import math
import jax
import jax.numpy as jnp
from jax import lax
from jax.sharding import PartitionSpec as P

DH = 96
LBLOCK = 256
eps_norm = 1e-06


def passed_along(value, axis, steps):
    count = lax.axis_size(axis)
    initial, last = (max(0, -steps), min(count, count - steps))
    return lax.ppermute(value, axis, [(source, source + steps) for source in range(initial, last)])


def block_step(carry_state, pieces):
    query_part, key_part, value_part, decay_part = pieces
    block_len = decay_part.shape[0]
    running = jnp.cumsum(decay_part, axis=0)
    by_head = running.T
    gaps_log = by_head[:, :, None] - by_head[:, None, :]
    causal = jnp.arange(block_len)[:, None] >= jnp.arange(block_len)[None, :]
    weight = jnp.exp(jnp.where(causal[None], gaps_log, -jnp.inf))
    scores = jnp.einsum("ihd,jhd->hij", query_part, key_part, preferred_element_type=jnp.float32)
    mixing = (scores * weight).astype(jnp.bfloat16)
    inside = jnp.einsum("hij,jhd->ihd", mixing, value_part, preferred_element_type=jnp.float32)
    outside = jnp.einsum(
        "ihd,hde->ihe",
        query_part.astype(jnp.float32) * jnp.exp(running)[:, :, None],
        carry_state,
        precision=lax.Precision.HIGHEST,
    )
    block_total = running[-1]
    update = jnp.einsum(
        "jhd,jhe->hde",
        key_part.astype(jnp.float32) * jnp.exp(block_total[None, :] - running)[:, :, None],
        value_part.astype(jnp.float32),
        precision=lax.Precision.HIGHEST,
    )
    new_state = jnp.exp(block_total)[:, None, None] * carry_state + update
    return (new_state, inside + outside)


def per_device(query1, key1, value1, log_decay, out_weight, query2, key2, value2):
    tok_rows = query1.shape[0]
    head_count = log_decay.shape[1]
    head_size = DH
    block_count = tok_rows // LBLOCK
    inputs = (
        query1.reshape(block_count, LBLOCK, head_count, head_size),
        key1.reshape(block_count, LBLOCK, head_count, head_size),
        value1.reshape(block_count, LBLOCK, head_count, head_size),
        log_decay.reshape(block_count, LBLOCK, head_count),
    )
    empty_state = jnp.zeros((head_count, head_size, head_size), jnp.float32)
    state_dev, outputs = lax.scan(block_step, empty_state, inputs)
    local_out = outputs.reshape(tok_rows, head_count, head_size)
    decay_dev = jnp.cumsum(log_decay, axis=0)
    device_total = decay_dev[-1]
    position = lax.axis_index("ctx")
    totals = lax.all_gather(device_total[None, :], "ctx", axis=0, tiled=True)
    device_ids = jnp.arange(totals.shape[0], dtype=jnp.int32)[:, None]
    earlier_rows = device_ids < position
    running = jnp.cumsum(totals, axis=0)
    before_sum = jnp.sum(jnp.where(earlier_rows, totals, 0.0), axis=0)
    weights = jnp.exp(jnp.where(earlier_rows, before_sum[None, :] - running, -jnp.inf))
    incoming = empty_state + jnp.einsum(
        "nh,nhde->hde",
        weights,
        lax.all_gather(state_dev[None].astype(jnp.bfloat16), "ctx", axis=0, tiled=True).astype(
            jnp.float32
        ),
        precision=lax.Precision.HIGHEST,
    )
    correction = jnp.einsum(
        "ihd,hde->ihe",
        query1.reshape(tok_rows, head_count, head_size).astype(jnp.float32)
        * jnp.exp(decay_dev)[:, :, None],
        incoming,
        precision=lax.Precision.HIGHEST,
    )
    combined = local_out + correction
    mean_square = jnp.mean(combined * combined, axis=-1, keepdims=True)
    normed = (
        (combined / jnp.sqrt(mean_square + eps_norm))
        .astype(jnp.bfloat16)
        .reshape(tok_rows, head_count * head_size)
    )
    linear_mixed = lax.psum_scatter(
        jnp.dot(normed, out_weight, preferred_element_type=jnp.float32).astype(jnp.bfloat16),
        "head",
        scatter_dimension=0,
        tiled=True,
    )
    stacked = jnp.stack((key2, value2))
    received = []
    moving = stacked
    for distance in range(3):
        moving = passed_along(moving, "ctx", 1)
        received.append(moving)
    window_keys = jnp.concatenate([received[2], received[1], received[0], stacked], axis=1)
    heads_soft = query2.shape[1] // head_size
    query_rows = min(512, tok_rows)
    key_span = 3 * tok_rows + query_rows
    score_scale = 1.0 / math.sqrt(DH)
    lowest_key = (3 - position) * tok_rows

    def attend_block(block_index):
        first_row = block_index * query_rows
        query_part = query2.reshape(query_rows, heads_soft, head_size)
        key_part = window_keys[0].reshape(key_span, heads_soft, head_size)
        value_part = window_keys[1].reshape(key_span, heads_soft, head_size)
        scores = (
            jnp.einsum("ihd,jhd->hij", query_part, key_part, preferred_element_type=jnp.float32)
            * score_scale
        )
        query_pos = first_row + jnp.arange(query_rows, dtype=jnp.int32)[:, None]
        key_pos = first_row + jnp.arange(key_span, dtype=jnp.int32)[None, :]
        allowed = (
            (key_pos > query_pos) & (key_pos <= 3 * tok_rows + query_pos) & (key_pos >= lowest_key)
        )
        scores = jnp.where(allowed[None], scores, -jnp.inf)
        row_peak = jnp.max(scores, axis=-1, keepdims=True)
        exponent = jnp.exp(scores - row_peak)
        probability = (exponent / jnp.sum(exponent, axis=-1, keepdims=True)).astype(jnp.bfloat16)
        result = jnp.einsum(
            "hij,jhd->ihd", probability, value_part, preferred_element_type=jnp.float32
        )
        return result.astype(jnp.bfloat16).reshape(query_rows, heads_soft * head_size)

    attended = lax.map(attend_block, jnp.arange(tok_rows // query_rows, dtype=jnp.int32))
    attended = attended.reshape(tok_rows, heads_soft * head_size)
    return (linear_mixed, attended)


def solution(mesh):
    in_specs = (
        P("ctx", "head"),
        P("ctx", "head"),
        P("ctx", "head"),
        P("ctx", "head"),
        P("head", None),
        P("ctx", "head"),
        P("ctx", "head"),
        P("ctx", "head"),
    )
    out_specs = (P(("ctx", "head"), None), P("ctx", "head"))
    return jax.shard_map(
        per_device, mesh=mesh, in_specs=in_specs, out_specs=out_specs, check_vma=False
    )
```

profile of v0, /device:TPU:1, one launch (start us, length us, event | category | flops | bytes accessed | tf_op | source)
XLA Modules:
  0.0 302.6 jit_solution(10613626920884037711)
XLA Ops:
  7.2 2.2 reshape.198
  10.2 2.2 reshape.199
  13.1 3.0 reshape.200
  16.1 1.6 copy.60
  17.8 51.9 %while.4 = (s32[]{:T(128)}, f32[8,96,96]{2,1,0:T(8,128)S(1)}, f32[2,256,8,96]{1,0,3,2:T(2,128)}, f32[2,256,8]{1,2,0:T(8,128)}, bf16[2,256,8,96]{1,3,2,0:T(8,128)...) while((s32[]{:T(128)}, f32[8,96,96]{2,1,0:T(8,128)S(1)}, ...), condition=%wide.region_3.4_spmd.clone, body=%wide.region_0.3_spmd.clone.sunk | while | flops 658018304 | bytes 9203808 | solution.py:58
  20.5 1.7 fusion.98
  23.6 1.7 fusion.99
  26.1 16.7 %dynamic_update_slice.9 = f32[2,256,8,96]{1,0,3,2:T(2,128)} dynamic-update-slice(f32[2,256,8,96]{1,0,3,2:T(2,128)} %get-tuple-element.191, f32[1,256,8,96]{1,0,3,2:T(1,128)S(1)} %copy.94, s32[]{:T(128)} %get-tuple-element.189, s32[]{:T(128)} %constant.60.clone.1..sunk, s32[]{:T(128)} %constant.60.clone.1..sunk, s32[]{:T(128)} %constant.60.clone.1..sunk) | dynamic-update-slice | bytes 1572868 | tf_op jit(solution)/shard_map/while/body/jit(dynamic_update_index_in_dim)/dynamic_update_slice | solution.py:58
  46.4 1.7 fusion.98
  49.5 1.7 fusion.99
  52.0 16.7 %dynamic_update_slice.9 = f32[2,256,8,96]{1,0,3,2:T(2,128)} dynamic-update-slice(f32[2,256,8,96]{1,0,3,2:T(2,128)} %get-tuple-element.191, f32[1,256,8,96]{1,0,3,2:T(1,128)S(1)} %copy.94, s32[]{:T(128)} %get-tuple-element.189, s32[]{:T(128)} %constant.60.clone.1..sunk, s32[]{:T(128)} %constant.60.clone.1..sunk, s32[]{:T(128)} %constant.60.clone.1..sunk) | dynamic-update-slice | bytes 1572868 | tf_op jit(solution)/shard_map/while/body/jit(dynamic_update_index_in_dim)/dynamic_update_slice | solution.py:58
  70.5 2.7 pad_maximum_fusion
  73.2 6.2 %collective-permute-start = (bf16[2,512,768]{2,1,0:T(8,128)(2,1)}, bf16[2,512,768]{2,1,0:T(8,128)(2,1)}, u32[]{:S(2)}, u32[]{:S(2)}) collective-permute-start(bf16[2,512,768]{2,1,0:T(8,128)(2,1)} %pad_maximum_fusion), channel_id=1, source_target_pairs={{0,8},{8,16},{16,24},{24,32},{32,40},{40,48},{48,56},{56,64},{64,7... | collective-permute-start | bytes 4718600 | tf_op jit(solution)/shard_map/ppermute | solution.py:15
  79.7 2.2 reduce-window.16
  82.3 52.6 %all-gather.1 = f32[32,1,8]{2,1,0:T(1,128)S(1)} all-gather(f32[1,1,8]{2,1,0:T(1,128)S(1)} %bitcast.146), channel_id=1, replica_groups=mesh['ctx'=32,'head'=8] {'ctx'}, dimensions={0}, use_global_device_ids=true | all-gather | bytes 1056 | tf_op jit(solution)/shard_map/all_gather | solution.py:63
  135.0 2.5 reshape.184
  137.8 2.1 collective-permute-start.1
  139.9 45.3 %all-gather.4.cloned.1.call-done = bf16[256,96,96]{2,1,0:T(8,128)(2,1)} async-done(((bf16[8,96,96]{2,1,0:T(8,128)(2,1)}), bf16[256,96,96]{2,1,0:T(8,128)(2,1)}) %all-gather.4.cloned.1.call-update) | async-done | bytes 4718608 | tf_op jit(solution)/shard_map/all_gather | solution.py:72
  185.1 4.5 %multiply_reduce_fusion = f32[8,96,96]{2,1,0:T(8,128)S(1)} fusion(bf16[8,32,96,96]{3,2,0,1:T(8,128)(2,1)} %bitcast.131, f32[8,32]{0,1:T(8,128)S(1)} %exponential_bitcast_fusion), kind=kLoop, calls=%fused_computation.53 | loop fusion | flops 7004160 | bytes 5014528 | tf_op jit(solution)/shard_map/nh,nhde->hde/dot_general | solution.py:69
  189.6 1.6 multiply_reduce_fusion.1
  191.5 6.4 %convolution_convert_fusion = bf16[512,3072]{1,0:T(8,128)(2,1)} fusion(bf16[512,768]{0,1:T(8,128)(2,1)S(1)} %bitcast.143, bf16[768,3072]{1,0:T(8,128)(2,1)} %param.14), kind=kOutput, calls=%fused_computation.57 | convolution fusion | flops 2417491968 | bytes 8650752 | tf_op jit(solution)/shard_map/dot_general | solution.py:92
  197.9 2.1 collective-permute-start.2
  200.0 2.3 copy.65
  202.3 2.0 fusion.46
  204.3 42.8 %collective-permute-done.2 = bf16[2,512,768]{2,1,0:T(8,128)(2,1)S(1)} collective-permute-done((bf16[2,512,768]{2,1,0:T(8,128)(2,1)}, bf16[2,512,768]{2,1,0:T(8,128)(2,1)S(1)}, u32[]{:S(2)}, u32[]{:S(2)}) %collective-permute-start.2) | collective-permute-done | bytes 1572896 | tf_op jit(solution)/shard_map/ppermute | solution.py:15
  247.1 2.8 maximum_maximum_fusion
  249.9 2.1 fusion.66
  252.0 4.7 %copy.64 = bf16[1,2048,768]{1,2,0:T(8,128)(2,1)} copy(bf16[1,2048,768]{2,1,0:T(8,128)(2,1)} %get-tuple-element.128) | data formatting | bytes 6291456 | tf_op jit(solution)/shard_map/while/body/eval_jaxpr/slice | solution.py:113
  256.7 3.0 copy.63
  259.7 14.4 %fusion.67 = f32[8,512]{1,0:T(8,128)S(1)} fusion(pred[512,2048]{0,1:T(8,128)(4,1)} %fusion.46, bf16[2048,8,96]{0,2,1:T(8,128)(2,1)} %bitcast.132, bf16[512,8,96]{0,2,1:T(8,128)(2,1)} %bitcast.140), kind=kOutput, calls=%fused_computation.85 | convolution fusion | flops 1644169216 | bytes 4997120 | tf_op jit(solution)/shard_map/while/body/eval_jaxpr/sub | solution.py:126
  274.2 19.3 %fusion.54 = bf16[8,96,512]{2,1,0:T(8,128)(2,1)} fusion(bf16[2048,8,96]{0,2,1:T(8,128)(2,1)S(1)} %bitcast.134, f32[8,512]{1,0:T(8,128)S(1)} %fusion.67, pred[512,2048]{0,1:T(8,128)(4,1)} %fusion.46, bf16[2048,8,96]{0,2,1:T(8,128)(2,1)} %bitcast.133, bf16[512,8,96]{0,2,1:T(8,128)(2,1)} %bitcast.141), kind=kOutput, calls=%fused_computation.67 | convolution fusion | flops 3263567872 | bytes 8929280 | tf_op jit(solution)/shard_map/while/body/eval_jaxpr/hij,jhd->ihd/dot_general | solution.py:128
  293.5 2.3 copy.67
  (64 shorter events, 15.1 us)
Async XLA Ops:
  7.2 178.0 %all-gather.4.cloned.1.call-start = ((), (), s32[]{:S(2)}) async-start(), calls=%async_computation.2 | async-start | bytes 6488064 | tf_op jit(solution)/shard_map/all_gather | solution.py:72
  19.3 0.6 copy-start.4
  45.2 0.6 copy-start.4
  69.7 9.7 %copy-start = (bf16[512,768]{1,0:T(8,128)(2,1)S(1)}, bf16[512,768]{1,0:T(8,128)(2,1)}, u32[]{:S(2)}) copy-start(bf16[512,768]{1,0:T(8,128)(2,1)} %param.10) | copy-start | bytes 2359300
  70.4 225.3 %reduce-scatter.2.cloned.1.call-start = ((), (), s32[]{:S(2)}) async-start(), calls=%async_computation.1 | async-start | bytes 3538944 | tf_op jit(solution)/shard_map/reduce_scatter | solution.py:91
  73.2 64.6 %collective-permute-start = (bf16[2,512,768]{2,1,0:T(8,128)(2,1)}, bf16[2,512,768]{2,1,0:T(8,128)(2,1)}, u32[]{:S(2)}, u32[]{:S(2)}) collective-permute-start(bf16[2,512,768]{2,1,0:T(8,128)(2,1)} %pad_maximum_fusion), channel_id=1, source_target_pairs={{0,8},{8,16},{16,24},{24,32},{32,40},{40,48},{48,56},{56,64},{64,7... | collective-permute-start | bytes 4718600 | tf_op jit(solution)/shard_map/ppermute | solution.py:15
  137.8 60.1 %collective-permute-start.1 = (bf16[2,512,768]{2,1,0:T(8,128)(2,1)}, bf16[2,512,768]{2,1,0:T(8,128)(2,1)}, u32[]{:S(2)}, u32[]{:S(2)}) collective-permute-start(bf16[2,512,768]{2,1,0:T(8,128)(2,1)} %collective-permute-done), channel_id=1, source_target_pairs={{0,8},{8,16},{16,24},{24,32},{32,40},{40,48},{48,56},{56,64},{64,7... | collective-permute-start | bytes 4718600 | tf_op jit(solution)/shard_map/ppermute | solution.py:15
  197.9 49.2 %copy-start.2 = (bf16[512,768]{1,0:T(8,128)(2,1)S(1)}, bf16[512,768]{1,0:T(8,128)(2,1)}, u32[]{:S(2)}) copy-start(bf16[512,768]{1,0:T(8,128)(2,1)} %param.17) | copy-start | bytes 2359300
  197.9 49.2 %copy-start.3 = (bf16[512,768]{1,0:T(8,128)(2,1)S(1)}, bf16[512,768]{1,0:T(8,128)(2,1)}, u32[]{:S(2)}) copy-start(bf16[512,768]{1,0:T(8,128)(2,1)} %param.16) | copy-start | bytes 2359300
  197.9 49.2 %collective-permute-start.2 = (bf16[2,512,768]{2,1,0:T(8,128)(2,1)}, bf16[2,512,768]{2,1,0:T(8,128)(2,1)S(1)}, u32[]{:S(2)}, u32[]{:S(2)}) collective-permute-start(bf16[2,512,768]{2,1,0:T(8,128)(2,1)} %collective-permute-done.1), channel_id=1, source_target_pairs={{0,8},{8,16},{16,24},{24,32},{32,40},{40,48},{48,56},{56,64},{64,7... | collective-permute-start | bytes 4718600 | tf_op jit(solution)/shard_map/ppermute | solution.py:15
  259.7 14.4 %copy-start.1 = (bf16[1,2048,768]{1,2,0:T(8,128)(2,1)S(1)}, bf16[1,2048,768]{1,2,0:T(8,128)(2,1)}, u32[]{:S(2)}) copy-start(bf16[1,2048,768]{1,2,0:T(8,128)(2,1)} %copy.63) | copy-start | bytes 9437188
Sparse Core Ops, SparseCore 0:
  70.5 114.5 all-gather.3
  198.0 39.6 reduce-scatter.1
where the time goes:
time: 306 us; the launch traced here: 303 us
  waiting for transfers between devices  88.1 us (29%)
  local copies, waits for them, and re-layouts  66.2 us (22%)
  blocking collectives  52.6 us (17%)
  matrix products  49.9 us (16%)
  other arithmetic  21 us (7%)
  between operations  14.2 us (5%)
  starting transfers between devices  10.4 us (3%)
    all_gather x1, blocking collectives, per_device(): totals = lax.all_gather(device_total[None, :], 'ctx', axis=0, tiled=True)  52.6 us
    all_gather x1, waiting for transfers between devices, per_device(): lax.all_gather(state_dev[None].astype(jnp.bfloat16), 'ctx', axis=0, tiled...  45.3 us
    ppermute x3, waiting for transfers between devices, passed_along(): lax.ppermute(value, axis, [(source, source + steps) for source in range(i...  42.9 us
    dynamic_update_slice x4, local copies, waits for them, and re-layouts, per_device(): state_dev, outputs = lax.scan(block_step, empty_state, inputs)  35 us
    dot_general x1, matrix products, attend_block(): jnp.einsum('hij,jhd->ihd', probability, value_part, preferred_element_typ...  19.3 us
    sub x1, matrix products, attend_block(): exponent = jnp.exp(scores - row_peak)  14.4 us
    ppermute x3, starting transfers between devices, passed_along(): lax.ppermute(value, axis, [(source, source + steps) for source in range(i...  10.3 us
    unnamed x14, local copies, waits for them, and re-layouts  7.93 us
  transfers between devices with their start and end apart: 5, of which 2 were waited for; matrix products, arithmetic and copies ran while one was open for 24% of the time, Pallas kernels for 0%

commit v1 on v0

--- a/solution.py
+++ b/solution.py
@@ -60,7 +60,16 @@
     decay_dev = jnp.cumsum(log_decay, axis=0)
     device_total = decay_dev[-1]
     position = lax.axis_index("ctx")
-    totals = lax.all_gather(device_total[None, :], "ctx", axis=0, tiled=True)
+    local = device_total[None, :]
+    totals = jnp.concatenate(
+        jax.lax.all_to_all(
+            jnp.stack([local] * jax.lax.psum(1, axis_name="ctx")),
+            axis_name="ctx",
+            split_axis=0,
+            concat_axis=0,
+        ),
+        0,
+    )
     device_ids = jnp.arange(totals.shape[0], dtype=jnp.int32)[:, None]
     earlier_rows = device_ids < position
     running = jnp.cumsum(totals, axis=0)

time: 306 us -> 294 us (0.961)
  blocking collectives: 52.6 us -> 0 us
  waiting for transfers between devices: 88.1 us -> 118 us
  starting transfers between devices: 10.4 us -> 20.3 us
    all_gather x1 -> x0, blocking collectives: 52.6 us -> none  [per_device(): totals = lax.all_gather(device_total[None, :], 'ctx', axis=0, tiled=True)]
    all_to_all x0 -> x1, waiting for transfers between devices: none -> 15.2 us  [per_device(): jax.lax.all_to_all(jnp.stack([local] * jax.lax.psum(1, axis_name='ctx')),...]
    all_gather x1, waiting for transfers between devices: 45.3 us -> 59.9 us  [per_device(): lax.all_gather(state_dev[None].astype(jnp.bfloat16), 'ctx', axis=0, tiled...]
    all_to_all x0 -> x1, starting transfers between devices: none -> 8.96 us  [per_device(): jax.lax.all_to_all(jnp.stack([local] * jax.lax.psum(1, axis_name='ctx')),...]
  transfers between devices with their start and end apart: 5 -> 6, of which waited for: 2 -> 3; matrix products, arithmetic and copies ran while one was open for 24% -> 26% of each run, Pallas kernels for 0% -> 0%
where the time goes in v1:
time: 294 us; the launch traced here: 290 us
  waiting for transfers between devices  118 us (40%)
  local copies, waits for them, and re-layouts  66.8 us (23%)
  matrix products  49.9 us (17%)
  other arithmetic  21 us (7%)
  starting transfers between devices  20.3 us (7%)
  between operations  14.3 us (5%)
    all_gather x1, waiting for transfers between devices, per_device(): lax.all_gather(state_dev[None].astype(jnp.bfloat16), 'ctx', axis=0, tiled...  59.9 us
    ppermute x3, waiting for transfers between devices, passed_along(): lax.ppermute(value, axis, [(source, source + steps) for source in range(i...  42.8 us
    dynamic_update_slice x4, local copies, waits for them, and re-layouts, per_device(): state_dev, outputs = lax.scan(block_step, empty_state, inputs)  35 us
    dot_general x1, matrix products, attend_block(): jnp.einsum('hij,jhd->ihd', probability, value_part, preferred_element_typ...  19.3 us
    all_to_all x1, waiting for transfers between devices, per_device(): jax.lax.all_to_all(jnp.stack([local] * jax.lax.psum(1, axis_name='ctx')),...  15.2 us
    sub x1, matrix products, attend_block(): exponent = jnp.exp(scores - row_peak)  14.4 us
    ppermute x3, starting transfers between devices, passed_along(): lax.ppermute(value, axis, [(source, source + steps) for source in range(i...  11.3 us
    all_to_all x1, starting transfers between devices, per_device(): jax.lax.all_to_all(jnp.stack([local] * jax.lax.psum(1, axis_name='ctx')),...  8.96 us
  transfers between devices with their start and end apart: 6, of which 3 were waited for; matrix products, arithmetic and copies ran while one was open for 26% of the time, Pallas kernels for 0%

profile of v1, /device:TPU:1, one launch (start us, length us, event | category | flops | bytes accessed | tf_op | source)
XLA Modules:
  0.0 290.3 jit_solution(1802006850435013422)
XLA Ops:
  7.2 2.2 reshape.203
  10.2 2.2 reshape.204
  13.1 3.0 %reshape.205 = bf16[2,256,8,96]{3,2,1,0:T(8,128)(2,1)} reshape(bf16[512,768]{1,0:T(8,128)(2,1)} %param.10) | data formatting | bytes 1572864 | tf_op jit(solution)/shard_map/reshape | solution.py:52
  16.1 1.6 copy.57
  17.8 51.9 %while.4 = (s32[]{:T(128)}, f32[8,96,96]{2,1,0:T(8,128)S(1)}, f32[2,256,8,96]{1,0,3,2:T(2,128)}, f32[2,256,8]{1,2,0:T(8,128)}, bf16[2,256,8,96]{1,3,2,0:T(8,128)...) while((s32[]{:T(128)}, f32[8,96,96]{2,1,0:T(8,128)S(1)}, ...), condition=%wide.region_3.4_spmd.clone, body=%wide.region_0.3_spmd.clone.sunk | while | flops 658018304 | bytes 9203808 | solution.py:58
  20.5 1.7 fusion.98
  23.6 1.7 fusion.99
  26.1 16.7 %dynamic_update_slice.9 = f32[2,256,8,96]{1,0,3,2:T(2,128)} dynamic-update-slice(f32[2,256,8,96]{1,0,3,2:T(2,128)} %get-tuple-element.191, f32[1,256,8,96]{1,0,3,2:T(1,128)S(1)} %copy.91, s32[]{:T(128)} %get-tuple-element.189, s32[]{:T(128)} %constant.60.clone.1..sunk, s32[]{:T(128)} %constant.60.clone.1..sunk, s32[]{:T(128)} %constant.60.clone.1..sunk) | dynamic-update-slice | bytes 1572868 | tf_op jit(solution)/shard_map/while/body/jit(dynamic_update_index_in_dim)/dynamic_update_slice | solution.py:58
  46.4 1.7 fusion.98
  49.5 1.7 fusion.99
  52.0 16.7 %dynamic_update_slice.9 = f32[2,256,8,96]{1,0,3,2:T(2,128)} dynamic-update-slice(f32[2,256,8,96]{1,0,3,2:T(2,128)} %get-tuple-element.191, f32[1,256,8,96]{1,0,3,2:T(1,128)S(1)} %copy.91, s32[]{:T(128)} %get-tuple-element.189, s32[]{:T(128)} %constant.60.clone.1..sunk, s32[]{:T(128)} %constant.60.clone.1..sunk, s32[]{:T(128)} %constant.60.clone.1..sunk) | dynamic-update-slice | bytes 1572868 | tf_op jit(solution)/shard_map/while/body/jit(dynamic_update_index_in_dim)/dynamic_update_slice | solution.py:58
  70.4 2.7 pad_maximum_fusion
  73.1 6.2 %collective-permute-start = (bf16[2,512,768]{2,1,0:T(8,128)(2,1)}, bf16[2,512,768]{2,1,0:T(8,128)(2,1)}, u32[]{:S(2)}, u32[]{:S(2)}) collective-permute-start(bf16[2,512,768]{2,1,0:T(8,128)(2,1)} %pad_maximum_fusion), channel_id=1, source_target_pairs={{0,8},{8,16},{16,24},{24,32},{32,40},{40,48},{48,56},{56,64},{64,7... | collective-permute-start | bytes 4718600 | tf_op jit(solution)/shard_map/ppermute | solution.py:15
  79.3 2.2 reduce-window.16
  82.6 9.0 %all-to-all-start = ((f32[32,1,8]{2,1,0:T(1,128)}), f32[32,1,8]{2,1,0:T(1,128)S(1)}, u32[]{:S(2)}, u32[]{:S(2)}) async-start(f32[32,1,8]{2,1,0:T(1,128)} %stack.12), calls=%async_computation | async-start | bytes 32768 | tf_op jit(solution)/shard_map/all_to_all | solution.py:65
  91.9 2.5 reshape.190
  94.5 15.2 %all-to-all-done = f32[32,1,8]{2,1,0:T(1,128)S(1)} async-done(((f32[32,1,8]{2,1,0:T(1,128)}), f32[32,1,8]{2,1,0:T(1,128)S(1)}, u32[]{:S(2)}, u32[]{:S(2)}) %all-to-all-start) | async-done | bytes 1056 | tf_op jit(solution)/shard_map/all_to_all | solution.py:65
  109.9 3.0 %collective-permute-start.1 = (bf16[2,512,768]{2,1,0:T(8,128)(2,1)}, bf16[2,512,768]{2,1,0:T(8,128)(2,1)}, u32[]{:S(2)}, u32[]{:S(2)}) collective-permute-start(bf16[2,512,768]{2,1,0:T(8,128)(2,1)} %collective-permute-done), channel_id=1, source_target_pairs={{0,8},{8,16},{16,24},{24,32},{32,40},{40,48},{48,56},{56,64},{64,7... | collective-permute-start | bytes 4718600 | tf_op jit(solution)/shard_map/ppermute | solution.py:15
  112.9 59.9 %all-gather.3.cloned.1.call-done = bf16[256,96,96]{2,1,0:T(8,128)(2,1)} async-done(((bf16[8,96,96]{2,1,0:T(8,128)(2,1)}), bf16[256,96,96]{2,1,0:T(8,128)(2,1)}) %all-gather.3.cloned.1.call-update) | async-done | bytes 4718608 | tf_op jit(solution)/shard_map/all_gather | solution.py:81
  172.8 4.5 %multiply_reduce_fusion = f32[8,96,96]{2,1,0:T(8,128)S(1)} fusion(bf16[8,32,96,96]{3,2,0,1:T(8,128)(2,1)} %bitcast.130, f32[8,32]{0,1:T(8,128)S(1)} %exponential_bitcast_fusion), kind=kLoop, calls=%fused_computation.53 | loop fusion | flops 7004160 | bytes 5014528 | tf_op jit(solution)/shard_map/nh,nhde->hde/dot_general | solution.py:78
  179.2 6.4 %convolution_convert_fusion = bf16[512,3072]{1,0:T(8,128)(2,1)} fusion(bf16[512,768]{0,1:T(8,128)(2,1)S(1)} %bitcast.142, bf16[768,3072]{1,0:T(8,128)(2,1)} %param.14), kind=kOutput, calls=%fused_computation.57 | convolution fusion | flops 2417491968 | bytes 8650752 | tf_op jit(solution)/shard_map/dot_general | solution.py:101
  185.6 2.1 collective-permute-start.2
  187.7 2.3 copy.62
  190.0 2.0 fusion.46
  192.0 42.8 %collective-permute-done.2 = bf16[2,512,768]{2,1,0:T(8,128)(2,1)S(1)} collective-permute-done((bf16[2,512,768]{2,1,0:T(8,128)(2,1)}, bf16[2,512,768]{2,1,0:T(8,128)(2,1)S(1)}, u32[]{:S(2)}, u32[]{:S(2)}) %collective-permute-start.2) | collective-permute-done | bytes 1572896 | tf_op jit(solution)/shard_map/ppermute | solution.py:15
  234.8 2.8 maximum_maximum_fusion
  237.6 2.1 fusion.66
  239.7 4.7 %copy.61 = bf16[1,2048,768]{1,2,0:T(8,128)(2,1)} copy(bf16[1,2048,768]{2,1,0:T(8,128)(2,1)} %get-tuple-element.128) | data formatting | bytes 6291456 | tf_op jit(solution)/shard_map/while/body/eval_jaxpr/slice | solution.py:122
  244.5 3.0 %copy.60 = bf16[1,2048,768]{1,2,0:T(8,128)(2,1)} copy(bf16[1,2048,768]{2,1,0:T(8,128)(2,1)S(1)} %get-tuple-element.129) | data formatting | bytes 6291456 | tf_op jit(solution)/shard_map/while/body/eval_jaxpr/slice | solution.py:123
  247.4 14.4 %fusion.67 = f32[8,512]{1,0:T(8,128)S(1)} fusion(pred[512,2048]{0,1:T(8,128)(4,1)} %fusion.46, bf16[2048,8,96]{0,2,1:T(8,128)(2,1)} %bitcast.131, bf16[512,8,96]{0,2,1:T(8,128)(2,1)} %bitcast.139), kind=kOutput, calls=%fused_computation.85 | convolution fusion | flops 1644169216 | bytes 4997120 | tf_op jit(solution)/shard_map/while/body/eval_jaxpr/sub | solution.py:135
  261.9 19.3 %fusion.54 = bf16[8,96,512]{2,1,0:T(8,128)(2,1)} fusion(bf16[2048,8,96]{0,2,1:T(8,128)(2,1)S(1)} %bitcast.133, f32[8,512]{1,0:T(8,128)S(1)} %fusion.67, pred[512,2048]{0,1:T(8,128)(4,1)} %fusion.46, bf16[2048,8,96]{0,2,1:T(8,128)(2,1)} %bitcast.132, bf16[512,8,96]{0,2,1:T(8,128)(2,1)} %bitcast.140), kind=kOutput, calls=%fused_computation.67 | convolution fusion | flops 3263567872 | bytes 8929280 | tf_op jit(solution)/shard_map/while/body/eval_jaxpr/hij,jhd->ihd/dot_general | solution.py:137
  281.2 2.3 copy.64
  (66 shorter events, 17.4 us)
Async XLA Ops:
  7.2 165.7 %all-gather.3.cloned.1.call-start = ((), (), s32[]{:S(2)}) async-start(), calls=%async_computation.3 | async-start | bytes 6488064 | tf_op jit(solution)/shard_map/all_gather | solution.py:81
  19.3 0.6 copy-start.4
  45.2 0.6 copy-start.4
  69.7 22.0 %copy-start = (bf16[512,768]{1,0:T(8,128)(2,1)S(1)}, bf16[512,768]{1,0:T(8,128)(2,1)}, u32[]{:S(2)}) copy-start(bf16[512,768]{1,0:T(8,128)(2,1)} %param.10) | copy-start | bytes 2359300
  73.1 36.8 %collective-permute-start = (bf16[2,512,768]{2,1,0:T(8,128)(2,1)}, bf16[2,512,768]{2,1,0:T(8,128)(2,1)}, u32[]{:S(2)}, u32[]{:S(2)}) collective-permute-start(bf16[2,512,768]{2,1,0:T(8,128)(2,1)} %pad_maximum_fusion), channel_id=1, source_target_pairs={{0,8},{8,16},{16,24},{24,32},{32,40},{40,48},{48,56},{56,64},{64,7... | collective-permute-start | bytes 4718600 | tf_op jit(solution)/shard_map/ppermute | solution.py:15
  82.6 27.1 %all-to-all-start = ((f32[32,1,8]{2,1,0:T(1,128)}), f32[32,1,8]{2,1,0:T(1,128)S(1)}, u32[]{:S(2)}, u32[]{:S(2)}) async-start(f32[32,1,8]{2,1,0:T(1,128)} %stack.12), calls=%async_computation | async-start | bytes 32768 | tf_op jit(solution)/shard_map/all_to_all | solution.py:65
  91.6 191.9 %reduce-scatter.2.cloned.1.call-start = ((), (), s32[]{:S(2)}) async-start(), calls=%async_computation.2 | async-start | bytes 3538944 | tf_op jit(solution)/shard_map/reduce_scatter | solution.py:100
  109.9 75.7 %collective-permute-start.1 = (bf16[2,512,768]{2,1,0:T(8,128)(2,1)}, bf16[2,512,768]{2,1,0:T(8,128)(2,1)}, u32[]{:S(2)}, u32[]{:S(2)}) collective-permute-start(bf16[2,512,768]{2,1,0:T(8,128)(2,1)} %collective-permute-done), channel_id=1, source_target_pairs={{0,8},{8,16},{16,24},{24,32},{32,40},{40,48},{48,56},{56,64},{64,7... | collective-permute-start | bytes 4718600 | tf_op jit(solution)/shard_map/ppermute | solution.py:15
  185.6 49.2 %copy-start.2 = (bf16[512,768]{1,0:T(8,128)(2,1)S(1)}, bf16[512,768]{1,0:T(8,128)(2,1)}, u32[]{:S(2)}) copy-start(bf16[512,768]{1,0:T(8,128)(2,1)} %param.17) | copy-start | bytes 2359300
  185.6 49.2 %copy-start.3 = (bf16[512,768]{1,0:T(8,128)(2,1)S(1)}, bf16[512,768]{1,0:T(8,128)(2,1)}, u32[]{:S(2)}) copy-start(bf16[512,768]{1,0:T(8,128)(2,1)} %param.16) | copy-start | bytes 2359300
  185.6 49.2 %collective-permute-start.2 = (bf16[2,512,768]{2,1,0:T(8,128)(2,1)}, bf16[2,512,768]{2,1,0:T(8,128)(2,1)S(1)}, u32[]{:S(2)}, u32[]{:S(2)}) collective-permute-start(bf16[2,512,768]{2,1,0:T(8,128)(2,1)} %collective-permute-done.1), channel_id=1, source_target_pairs={{0,8},{8,16},{16,24},{24,32},{32,40},{40,48},{48,56},{56,64},{64,7... | collective-permute-start | bytes 4718600 | tf_op jit(solution)/shard_map/ppermute | solution.py:15
  247.4 14.4 %copy-start.1 = (bf16[1,2048,768]{1,2,0:T(8,128)(2,1)S(1)}, bf16[1,2048,768]{1,2,0:T(8,128)(2,1)}, u32[]{:S(2)}) copy-start(bf16[1,2048,768]{1,2,0:T(8,128)(2,1)} %copy.60) | copy-start | bytes 9437188
Sparse Core Ops, SparseCore 0:
  70.5 102.2 all-gather.2
  185.7 42.6 reduce-scatter.1
